TPU v7x, 128 devices: a whole 4x4x4 slice. The times are simulated.
128 devices in a mesh: fer: 8 (over z, y_hi), bos: 16 (over y_lo, x, core).
Axes of the slice: x: 4, y: 4 (y_hi: 2, y_lo: 2; y = y_hi * 2 + y_lo), z: 4, core: 2. Of those that a mesh axis runs over, the one named last changes fastest.
Arguments:
- green: bfloat16 [4, 64, 9, 64, 128], P(None, 'fer', None, 'bos'), may hold values from -6 to 6
- bos_weight: bfloat16 [128, 9, 64, 128], P('bos'), may hold values from -12 to 12
- vertex: float32 [64, 128], P('fer', 'bos'), may hold values from 0.25 to 1.75
- block_order: int32 [16], replicated, may hold values from 0 to 15, each once
- window_start: int32 [1], replicated, may hold values from 0 to 64
Outputs:
- sigma: float32 [64, 64, 9, 128], P('bos', 'fer')
Inputs may be any that keep to these rules, and one draw needn't show every extreme that they name: block_order holds every block number once.
All inputs are finite; a program needn't handle non-finite values.
Results may differ from a plain program's by a relative error of at most 0.0003.
Values may be sent and summed in bfloat16 or wider, within the bound.
A program may use at most 128 MiB of HBM per device.

v0:
```python
import math
import jax
import jax.numpy as jnp
from jax import lax
from jax.sharding import PartitionSpec as P

HIGHEST = lax.Precision.HIGHEST


def passed_along(array, axis, by):
    size = lax.axis_size(axis)
    return lax.ppermute(array, axis, [(i, (i + by) % size) for i in range(size)])


def trig_tables(length):
    index = jnp.arange(length, dtype=jnp.int32)
    phase = (index[:, None] * index[None, :] % length).astype(jnp.float32) * (
        2.0 * math.pi / length
    )
    return (jnp.cos(phase), jnp.sin(phase))


def row_matrix(length, forward):
    cosine, sine = trig_tables(length)
    if forward:
        upper = jnp.concatenate([cosine, -sine], axis=1)
        lower = jnp.concatenate([sine, cosine], axis=1)
        block = jnp.concatenate([upper, lower], axis=0)
    else:
        upper = jnp.concatenate([cosine, sine], axis=1)
        lower = jnp.concatenate([-sine, cosine], axis=1)
        block = jnp.concatenate([upper, lower], axis=0) / length
    turned = jnp.concatenate([block[:, length:], -block[:, :length]], axis=1)
    return jnp.concatenate([block, turned], axis=1)


def col_tables(length, forward):
    cosine, sine = trig_tables(length)
    if forward:
        return (cosine, sine)
    return (cosine / length, -sine / length)


def row_step(field, matrix):
    return jnp.einsum("...c,cd->...d", field, matrix, precision=HIGHEST)


def col_step(halves, cos_part, sin_part):
    width = halves.shape[-1] // 2
    first = jnp.einsum("ax,nmxc->nmac", cos_part, halves[..., :width], precision=HIGHEST)
    return first + jnp.einsum("ax,nmxc->nmac", sin_part, halves[..., width:], precision=HIGHEST)


def body(green, bos_weight, vertex, block_order, window_start):
    num_fer = lax.axis_size("fer")
    fer_index = lax.axis_index("fer")
    bos_index = lax.axis_index("bos")
    num_slot = green.shape[0]
    window_dev = green.shape[1]
    orbitals = int(round(math.sqrt(green.shape[2])))
    bos_dev = bos_weight.shape[0]
    rows_all = bos_weight.shape[2]
    half_width = bos_weight.shape[3] // 2
    block_id = lax.dynamic_index_in_dim(block_order, bos_index, 0, keepdims=False)
    offset = window_start[0] + block_id * bos_dev
    shift_blocks = offset // window_dev
    inner = offset % window_dev
    shift_bits = shift_blocks % num_fer
    forward_rows = row_matrix(half_width, True)
    inverse_rows = row_matrix(half_width, False)
    forward_cos, forward_sin = col_tables(rows_all, True)
    inverse_cos, inverse_sin = col_tables(rows_all, False)
    full_rows = lax.all_gather(green, "bos", axis=3, tiled=True)
    current = full_rows
    for level in range(num_fer.bit_length() - 1):
        moved = passed_along(current, "fer", -(1 << level))
        current = jnp.where((shift_bits >> level) % 2 == 1, moved, current)
    sources = [current]
    for extra in range(2):
        current = passed_along(current, "fer", -1)
        sources.append(current)
    picked = []
    for extra in range(3):
        slot = (fer_index + shift_blocks + extra) // num_fer % num_slot
        picked.append(lax.dynamic_index_in_dim(sources[extra], slot, 0, keepdims=False))
    blocks = jnp.concatenate(picked, axis=0)
    halves = row_step(blocks.astype(jnp.float32), forward_rows)
    green_real = col_step(halves, forward_cos, forward_sin)
    weight_real = col_step(
        row_step(bos_weight.astype(jnp.float32), inverse_rows), inverse_cos, inverse_sin
    )
    total = jnp.zeros((window_dev, orbitals * orbitals, rows_all, 2 * half_width), jnp.float32)
    for column in range(bos_dev):
        part = lax.dynamic_slice_in_dim(green_real, inner + column, window_dev, 0)
        part = part.reshape(window_dev, orbitals, orbitals, 1, rows_all, 2 * half_width)
        factor = weight_real[column].reshape(1, 1, orbitals, orbitals, rows_all, 2 * half_width)
        green_re, green_im = (part[..., :half_width], part[..., half_width:])
        weight_re, weight_im = (factor[..., :half_width], factor[..., half_width:])
        real_part = jnp.sum(green_re * weight_re - green_im * weight_im, axis=2)
        imag_part = jnp.sum(green_re * weight_im + green_im * weight_re, axis=2)
        product = jnp.concatenate([real_part, imag_part], axis=-1)
        product = product.reshape(window_dev, orbitals * orbitals, rows_all, 2 * half_width)
        total = total + vertex[:, column][:, None, None, None] * product
    sigma_halves = row_step(-total, inverse_rows)
    width = sigma_halves.shape[-1] // 2
    first = jnp.einsum("ax,nmxc->anmc", inverse_cos, sigma_halves[..., :width], precision=HIGHEST)
    return lax.psum_scatter(
        first
        + jnp.einsum("ax,nmxc->anmc", inverse_sin, sigma_halves[..., width:], precision=HIGHEST),
        "bos",
        scatter_dimension=0,
        tiled=True,
    )


def solution(mesh):
    return jax.shard_map(
        body,
        mesh=mesh,
        in_specs=(
            P(None, "fer", None, "bos", None),
            P("bos", None, None, None),
            P("fer", "bos"),
            P(),
            P(),
        ),
        out_specs=P("bos", "fer", None, None),
        check_vma=False,
    )
```

profile of v0, /device:TPU:0, one launch (start us, length us, event | category | flops | bytes accessed | tf_op | source)
XLA Modules:
  0.0 767.3 jit_solution(11547539962003725166)
XLA Ops:
  6.5 1.8 copy.12
  8.4 41.5 %all-gather.2.cloned.1.call-done = bf16[4,8,9,64,128]{4,1,2,0,3:T(8,128)(2,1)} async-done(((bf16[4,8,9,4,128]{4,1,2,0,3:T(8,128)(2,1)}), bf16[4,8,9,64,128]{4,1,2,0,3:T(8,128)(2,1)}) %all-gather.2.cloned.1.call-update) | async-done | bytes 4718608 | tf_op jit(solution)/shard_map/all_gather | solution.py:73
  50.0 5.1 collective-permute-start
  55.7 1.2 dynamic_slice.38
  57.6 99.2 %collective-permute-done = bf16[4,8,9,64,128]{4,1,2,0,3:T(8,128)(2,1)} collective-permute-done((bf16[4,8,9,64,128]{4,1,2,0,3:T(8,128)(2,1)}, bf16[4,8,9,64,128]{4,1,2,0,3:T(8,128)(2,1)}, u32[]{:S(2)}, u32[]{:S(2)}) %collective-permute-start) | collective-permute-done | bytes 4718624 | tf_op jit(solution)/shard_map/ppermute | solution.py:12
  156.8 5.0 broadcast_select_fusion
  161.8 1.9 collective-permute-start.1
  163.7 101.6 %collective-permute-done.1 = bf16[4,8,9,64,128]{4,1,2,0,3:T(8,128)(2,1)} collective-permute-done((bf16[4,8,9,64,128]{4,1,2,0,3:T(8,128)(2,1)}, bf16[4,8,9,64,128]{4,1,2,0,3:T(8,128)(2,1)}, u32[]{:S(2)}, u32[]{:S(2)}) %collective-permute-start.1) | collective-permute-done | bytes 4718624 | tf_op jit(solution)/shard_map/ppermute | solution.py:12
  265.2 5.0 broadcast_select_fusion.1
  270.2 2.1 collective-permute-start.2
  272.3 102.0 %collective-permute-done.2 = bf16[4,8,9,64,128]{4,1,2,0,3:T(8,128)(2,1)} collective-permute-done((bf16[4,8,9,64,128]{4,1,2,0,3:T(8,128)(2,1)}, bf16[4,8,9,64,128]{4,1,2,0,3:T(8,128)(2,1)}, u32[]{:S(2)}, u32[]{:S(2)}) %collective-permute-start.2) | collective-permute-done | bytes 4718624 | tf_op jit(solution)/shard_map/ppermute | solution.py:12
  374.3 2.8 broadcast_select_fusion.2
  377.1 2.2 copy-done.13
  379.3 7.3 collective-permute-start.3
  386.6 98.8 %collective-permute-done.3 = bf16[4,8,9,64,128]{4,1,2,0,3:T(8,128)(2,1)} collective-permute-done((bf16[4,8,9,64,128]{4,1,2,0,3:T(8,128)(2,1)S(1)}, bf16[4,8,9,64,128]{4,1,2,0,3:T(8,128)(2,1)}, u32[]{:S(2)}, u32[]{:S(2)}) %collective-permute-start.3) | collective-permute-done | bytes 4718624 | tf_op jit(solution)/shard_map/ppermute | solution.py:12
  485.4 6.6 collective-permute-start.4
  492.1 0.7 slice_reduce_fusion.7
  493.4 2.1 convolution_bitcast_fusion
  495.5 2.4 fusion.17
  497.9 2.5 add_bitcast_fusion
  500.6 0.9 slice_bitcast_fusion.31
  501.5 0.9 slice_bitcast_fusion.29
  502.4 0.9 slice_bitcast_fusion.27
  503.3 0.9 slice_bitcast_fusion.25
  504.3 0.9 slice_bitcast_fusion.23
  505.2 0.9 slice_bitcast_fusion.21
  506.1 0.9 slice_bitcast_fusion.19
  507.1 1.4 constant_dynamic-slice_fusion.10
  508.8 1.4 constant_dynamic-slice_fusion.9
  510.5 79.8 %collective-permute-done.4 = bf16[4,8,9,64,128]{4,1,2,0,3:T(8,128)(2,1)} collective-permute-done((bf16[4,8,9,64,128]{4,1,2,0,3:T(8,128)(2,1)}, bf16[4,8,9,64,128]{4,1,2,0,3:T(8,128)(2,1)}, u32[]{:S(2)}, u32[]{:S(2)}) %collective-permute-start.4) | collective-permute-done | bytes 4718624 | tf_op jit(solution)/shard_map/ppermute | solution.py:12
  590.3 1.4 constant_dynamic-slice_fusion.8
  591.9 6.1 fusion.4
  598.0 5.0 copy-done.2
  603.1 7.3 fusion
  610.4 9.5 %fusion.10 = f32[24,9,128,64]{2,3,1,0:T(8,128)S(1)} fusion(f32[24,9,128,64]{2,3,1,0:T(8,128)S(1)} %fusion, f32[24,9,64,256]{3,2,1,0:T(8,128)} %copy-done.2), kind=kOutput, calls=%fused_computation.29 | convolution fusion | flops 1360781312 | bytes 21233664 | tf_op jit(solution)/shard_map/ax,nmxc->nmac/dot_general | solution.py:50
  619.9 4.7 constant_dynamic-slice_fusion.7
  624.6 4.8 slice_bitcast_fusion.15
  629.4 2.5 slice_bitcast_fusion.13
  631.8 3.1 slice_bitcast_fusion.11
  635.0 3.1 slice_bitcast_fusion.9
  638.1 2.3 slice_bitcast_fusion.7
  640.4 0.8 slice_bitcast_fusion.5
  641.2 0.8 slice_bitcast_fusion.3
  642.1 0.8 slice_bitcast_fusion.1
  643.0 0.8 copy-done.12
  643.9 3.7 subtract_reduce_fusion.7
  648.3 1.0 copy-done.11
  649.3 3.3 subtract_reduce_fusion.6
  653.3 0.9 copy-done.9
  654.3 0.7 copy-done.10
  655.1 3.3 subtract_reduce_fusion.5
  659.1 0.9 copy-done.7
  660.1 0.7 copy-done.8
  660.9 3.3 subtract_reduce_fusion.4
  664.9 1.0 copy-done.6
  665.9 3.5 subtract_reduce_fusion.3
  670.5 3.3 subtract_reduce_fusion.2
  674.7 3.3 subtract_reduce_fusion.1
  678.7 3.5 subtract_reduce_fusion
  683.1 4.8 fusion.21
  687.8 2.3 fusion.13
  690.2 2.4 fusion.40
  692.6 2.8 copy.16
  695.4 64.8 %reduce-scatter.2.cloned.1.call-done = f32[4,8,9,128]{3,1,2,0:T(8,128)} async-done(((f32[64,8,9,128]{3,1,2,0:T(8,128)}), f32[4,8,9,128]{3,1,2,0:T(8,128)}) %reduce-scatter.2.cloned.1.call-update) | async-done | bytes 147472 | tf_op jit(solution)/shard_map/reduce_scatter | solution.py:107
  (75 shorter events, 8.6 us)
Async XLA Ops:
  6.5 486.9 %copy-start = (bf16[8,9,64,128]{3,2,1,0:T(8,128)(2,1)S(1)}, bf16[8,9,64,128]{3,2,1,0:T(8,128)(2,1)}, u32[]{:S(2)}) copy-start(bf16[8,9,64,128]{3,2,1,0:T(8,128)(2,1)} %param.6) | copy-start | bytes 3538948
  6.5 43.4 %all-gather.2.cloned.1.call-start = ((), (), s32[]{:S(2)}) async-start(), calls=%async_computation.1 | async-start | bytes 5013504 | tf_op jit(solution)/shard_map/all_gather | solution.py:73
  8.4 751.9 %reduce-scatter.2.cloned.1.call-start = ((), (), s32[]{:S(2)}) async-start(), calls=%async_computation.2 | async-start | bytes 2506752 | tf_op jit(solution)/shard_map/reduce_scatter | solution.py:107
  50.0 106.8 %collective-permute-start = (bf16[4,8,9,64,128]{4,1,2,0,3:T(8,128)(2,1)}, bf16[4,8,9,64,128]{4,1,2,0,3:T(8,128)(2,1)}, u32[]{:S(2)}, u32[]{:S(2)}) collective-permute-start(bf16[4,8,9,64,128]{4,1,2,0,3:T(8,128)(2,1)} %all-gather.2.cloned.1.call-done), channel_id=1, source_target_pairs={{0,112},{16,0},{32,16},{48,32},{64,48},{80,64},{96,80},{112,96},{1... | collective-permute-start | bytes 14155784 | tf_op jit(solution)/shard_map/ppermute | solution.py:12
  161.8 103.4 %collective-permute-start.1 = (bf16[4,8,9,64,128]{4,1,2,0,3:T(8,128)(2,1)}, bf16[4,8,9,64,128]{4,1,2,0,3:T(8,128)(2,1)}, u32[]{:S(2)}, u32[]{:S(2)}) collective-permute-start(bf16[4,8,9,64,128]{4,1,2,0,3:T(8,128)(2,1)} %broadcast_select_fusion), channel_id=1, source_target_pairs={{0,96},{16,112},{32,0},{48,16},{64,32},{80,48},{96,64},{112,80},{1... | collective-permute-start | bytes 14155784 | tf_op jit(solution)/shard_map/ppermute | solution.py:12
  270.2 104.0 %collective-permute-start.2 = (bf16[4,8,9,64,128]{4,1,2,0,3:T(8,128)(2,1)}, bf16[4,8,9,64,128]{4,1,2,0,3:T(8,128)(2,1)}, u32[]{:S(2)}, u32[]{:S(2)}) collective-permute-start(bf16[4,8,9,64,128]{4,1,2,0,3:T(8,128)(2,1)} %broadcast_select_fusion.1), channel_id=1, source_target_pairs={{0,64},{16,80},{32,96},{48,112},{64,0},{80,16},{96,32},{112,48},{1... | collective-permute-start | bytes 14155784 | tf_op jit(solution)/shard_map/ppermute | solution.py:12
  272.3 219.8 %copy-start.29 = (f32[8,8]{1,0:T(8,128)S(1)}, f32[8,8]{1,0:T(8,128)}, u32[]{:S(2)}) copy-start(f32[8,8]{1,0:T(8,128)} %param.7) | copy-start | bytes 772
  377.1 2.2 copy-start.13
  379.3 106.1 %collective-permute-start.3 = (bf16[4,8,9,64,128]{4,1,2,0,3:T(8,128)(2,1)S(1)}, bf16[4,8,9,64,128]{4,1,2,0,3:T(8,128)(2,1)}, u32[]{:S(2)}, u32[]{:S(2)}) collective-permute-start(bf16[4,8,9,64,128]{4,1,2,0,3:T(8,128)(2,1)S(1)} %broadcast_select_fusion.2), channel_id=1, source_target_pairs={{0,112},{16,0},{32,16},{48,32},{64,48},{80,64},{96,80},{112,96},{1... | collective-permute-start | bytes 14155784 | tf_op jit(solution)/shard_map/ppermute | solution.py:12
  485.4 104.8 %collective-permute-start.4 = (bf16[4,8,9,64,128]{4,1,2,0,3:T(8,128)(2,1)}, bf16[4,8,9,64,128]{4,1,2,0,3:T(8,128)(2,1)}, u32[]{:S(2)}, u32[]{:S(2)}) collective-permute-start(bf16[4,8,9,64,128]{4,1,2,0,3:T(8,128)(2,1)} %collective-permute-done.3), channel_id=1, source_target_pairs={{0,112},{16,0},{32,16},{48,32},{64,48},{80,64},{96,80},{112,96},{1... | collective-permute-start | bytes 14155784 | tf_op jit(solution)/shard_map/ppermute | solution.py:12
  493.4 2.1 copy-start.27
  598.0 5.1 copy-start.2
  624.6 4.8 copy-start.5
  629.4 2.5 copy-start.4
  631.8 3.2 copy-start.3
  642.1 1.7 copy-start.12
  642.1 1.7 copy-start.25
  642.1 1.7 copy-start.26
  647.6 1.7 copy-start.11
  647.6 1.7 copy-start.23
  647.6 1.7 copy-start.24
  652.6 1.7 copy-start.9
  652.6 2.4 copy-start.10
  652.6 2.4 copy-start.21
  652.7 2.4 copy-start.22
  658.4 1.7 copy-start.7
  658.4 2.4 copy-start.8
  658.4 2.4 copy-start.19
  658.4 2.4 copy-start.20
  664.2 1.7 copy-start.6
  664.2 1.7 copy-start.17
  664.2 1.7 copy-start.18
  669.4 1.0 copy-start.15
  669.4 1.0 copy-start.16
  673.8 1.0 copy-start.14
  682.2 0.8 copy-start.28
  682.2 0.8 copy-start.30
  692.6 67.6 %copy-start.1 = (bf16[8,9,64,128]{3,2,1,0:T(8,128)(2,1)S(1)}, bf16[8,9,64,128]{3,2,1,0:T(8,128)(2,1)}, u32[]{:S(2)}) copy-start(bf16[8,9,64,128]{3,2,1,0:T(8,128)(2,1)} %param.6) | copy-start | bytes 3538948
Sparse Core Ops, SparseCore 0:
  9.1 40.8 all-gather.1
  695.6 64.6 reduce-scatter.1
where the time goes:
time: 771 us; the launch traced here: 767 us
  waiting for transfers between devices  588 us (76%)
  local copies, waits for them, and re-layouts  55.9 us (7%)
  other arithmetic  45.9 us (6%)
  matrix products  39.4 us (5%)
  starting transfers between devices  23 us (3%)
  between operations  15.5 us (2%)
    ppermute x5, waiting for transfers between devices, passed_along(): lax.ppermute(array, axis, [(i, (i + by) % size) for i in range(size)])  481 us
    reduce_scatter x1, waiting for transfers between devices, body(): lax.psum_scatter(first + jnp.einsum('ax,nmxc->anmc', inverse_sin, sigma_h...  64.8 us
    all_gather x1, waiting for transfers between devices, body(): full_rows = lax.all_gather(green, 'bos', axis=3, tiled=True)  41.5 us
    reduce_sum x8, other arithmetic, body(): real_part = jnp.sum(green_re * weight_re - green_im * weight_im, axis=2)  27.1 us
    mul x16, local copies, waits for them, and re-layouts, body(): real_part = jnp.sum(green_re * weight_re - green_im * weight_im, axis=2)  24.8 us
    ppermute x5, starting transfers between devices, passed_along(): lax.ppermute(array, axis, [(i, (i + by) % size) for i in range(size)])  22.9 us
    unnamed x63, local copies, waits for them, and re-layouts  16.4 us
  transfers between devices with their start and end apart: 7, of which 7 were waited for; matrix products, arithmetic and copies ran while one was open for 3% of the time, Pallas kernels for 0%

commit v1 on v0

--- a/solution.py
+++ b/solution.py
@@ -70,7 +70,9 @@
     inverse_rows = row_matrix(half_width, False)
     forward_cos, forward_sin = col_tables(rows_all, True)
     inverse_cos, inverse_sin = col_tables(rows_all, False)
-    full_rows = lax.all_gather(green, "bos", axis=3, tiled=True)
+    full_rows = jnp.concatenate(
+        lax.all_to_all(jnp.stack([green] * lax.axis_size("bos")), "bos", 0, 0), axis=3
+    )
     current = full_rows
     for level in range(num_fer.bit_length() - 1):
         moved = passed_along(current, "fer", -(1 << level))

time: 771 us -> 798 us (1.035)
  blocking collectives: 0 us -> 61.1 us
  waiting for transfers between devices: 588 us -> 548 us
    all_to_all x0 -> x1, blocking collectives: none -> 61.1 us  [body(): lax.all_to_all(jnp.stack([green] * lax.axis_size('bos')), 'bos', 0, 0)]
    all_gather x1 -> x0, waiting for transfers between devices: 41.5 us -> none  [body(): full_rows = lax.all_gather(green, 'bos', axis=3, tiled=True)]
    unnamed x63 -> x64, local copies, waits for them, and re-layouts: 16.4 us -> 14.6 us
  transfers between devices with their start and end apart: 7 -> 6, of which waited for: 7 -> 6; matrix products, arithmetic and copies ran while one was open for 3% -> 2% of each run, Pallas kernels for 0% -> 0%
where the time goes in v1:
time: 798 us; the launch traced here: 793 us
  waiting for transfers between devices  548 us (69%)
  blocking collectives  61.1 us (8%)
  local copies, waits for them, and re-layouts  59.7 us (7%)
  other arithmetic  45.8 us (6%)
  matrix products  39.4 us (5%)
  starting transfers between devices  23.5 us (3%)
  between operations  15.5 us (2%)
    ppermute x5, waiting for transfers between devices, passed_along(): lax.ppermute(array, axis, [(i, (i + by) % size) for i in range(size)])  478 us
    reduce_scatter x1, waiting for transfers between devices, body(): lax.psum_scatter(first + jnp.einsum('ax,nmxc->anmc', inverse_sin, sigma_h...  69.5 us
    all_to_all x1, blocking collectives, body(): lax.all_to_all(jnp.stack([green] * lax.axis_size('bos')), 'bos', 0, 0)  61.1 us
    reduce_sum x8, other arithmetic, body(): real_part = jnp.sum(green_re * weight_re - green_im * weight_im, axis=2)  27.1 us
    mul x16, local copies, waits for them, and re-layouts, body(): real_part = jnp.sum(green_re * weight_re - green_im * weight_im, axis=2)  24.8 us
    ppermute x5, starting transfers between devices, passed_along(): lax.ppermute(array, axis, [(i, (i + by) % size) for i in range(size)])  23.5 us
  transfers between devices with their start and end apart: 6, of which 6 were waited for; matrix products, arithmetic and copies ran while one was open for 2% of the time, Pallas kernels for 0%

profile of v1, /device:TPU:0, one launch (start us, length us, event | category | flops | bytes accessed | tf_op | source)
XLA Modules:
  0.0 792.8 jit_solution(11642520241592648476)
XLA Ops:
  6.5 2.9 stack.2
  9.4 61.1 %all_to_all.5 = bf16[16,4,8,9,4,128]{5,4,3,2,1,0:T(4,128)(2,1)S(1)} all-to-all(bf16[16,4,8,9,4,128]{5,4,3,2,1,0:T(4,128)(2,1)S(1)} %stack.2), channel_id=1, replica_groups=mesh['fer'=8,'bos'=16] {'bos'}, dimensions={0} | all-to-all | bytes 9437184 | tf_op jit(solution)/shard_map/all_to_all | solution.py:74
  70.5 3.5 copy.13
  74.0 6.4 collective-permute-start
  82.4 99.0 %collective-permute-done = bf16[4,8,9,64,128]{4,1,3,2,0:T(8,128)(2,1)} collective-permute-done((bf16[4,8,9,64,128]{4,1,3,2,0:T(8,128)(2,1)}, bf16[4,8,9,64,128]{4,1,3,2,0:T(8,128)(2,1)}, u32[]{:S(2)}, u32[]{:S(2)}) %collective-permute-start) | collective-permute-done | bytes 4718624 | tf_op jit(solution)/shard_map/ppermute | solution.py:12
  181.4 5.0 broadcast_select_fusion
  186.3 1.6 collective-permute-start.1
  188.0 100.9 %collective-permute-done.1 = bf16[4,8,9,64,128]{4,1,3,2,0:T(8,128)(2,1)} collective-permute-done((bf16[4,8,9,64,128]{4,1,3,2,0:T(8,128)(2,1)}, bf16[4,8,9,64,128]{4,1,3,2,0:T(8,128)(2,1)}, u32[]{:S(2)}, u32[]{:S(2)}) %collective-permute-start.1) | collective-permute-done | bytes 4718624 | tf_op jit(solution)/shard_map/ppermute | solution.py:12
  288.9 4.9 broadcast_select_fusion.1
  293.8 1.5 collective-permute-start.2
  295.3 101.6 %collective-permute-done.2 = bf16[4,8,9,64,128]{4,1,3,2,0:T(8,128)(2,1)} collective-permute-done((bf16[4,8,9,64,128]{4,1,3,2,0:T(8,128)(2,1)}, bf16[4,8,9,64,128]{4,1,3,2,0:T(8,128)(2,1)}, u32[]{:S(2)}, u32[]{:S(2)}) %collective-permute-start.2) | collective-permute-done | bytes 4718624 | tf_op jit(solution)/shard_map/ppermute | solution.py:12
  397.0 2.8 broadcast_select_fusion.2
  399.8 2.2 copy-done.13
  402.0 7.3 collective-permute-start.3
  409.3 97.9 %collective-permute-done.3 = bf16[4,8,9,64,128]{4,1,3,2,0:T(8,128)(2,1)} collective-permute-done((bf16[4,8,9,64,128]{4,1,3,2,0:T(8,128)(2,1)S(1)}, bf16[4,8,9,64,128]{4,1,3,2,0:T(8,128)(2,1)}, u32[]{:S(2)}, u32[]{:S(2)}) %collective-permute-start.3) | collective-permute-done | bytes 4718624 | tf_op jit(solution)/shard_map/ppermute | solution.py:12
  507.2 6.6 collective-permute-start.4
  513.9 0.7 slice_reduce_fusion.7
  515.2 2.1 convolution_bitcast_fusion
  517.3 2.4 fusion.17
  519.7 2.5 add_bitcast_fusion
  522.4 0.9 slice_bitcast_fusion.31
  523.3 0.9 slice_bitcast_fusion.29
  524.2 0.9 slice_bitcast_fusion.27
  525.1 0.9 slice_bitcast_fusion.25
  526.1 0.9 slice_bitcast_fusion.23
  527.0 0.9 slice_bitcast_fusion.21
  527.9 0.9 slice_bitcast_fusion.19
  528.9 1.4 constant_dynamic-slice_fusion.10
  530.6 1.4 constant_dynamic-slice_fusion.9
  532.2 78.9 %collective-permute-done.4 = bf16[4,8,9,64,128]{4,1,3,2,0:T(8,128)(2,1)} collective-permute-done((bf16[4,8,9,64,128]{4,1,3,2,0:T(8,128)(2,1)}, bf16[4,8,9,64,128]{4,1,3,2,0:T(8,128)(2,1)}, u32[]{:S(2)}, u32[]{:S(2)}) %collective-permute-start.4) | collective-permute-done | bytes 4718624 | tf_op jit(solution)/shard_map/ppermute | solution.py:12
  611.2 1.3 constant_dynamic-slice_fusion.8
  612.8 6.1 fusion.4
  618.9 5.0 copy-done.2
  623.9 7.3 fusion
  631.3 9.5 %fusion.10 = f32[24,9,128,64]{2,3,1,0:T(8,128)S(1)} fusion(f32[24,9,128,64]{2,3,1,0:T(8,128)S(1)} %fusion, f32[24,9,64,256]{3,2,1,0:T(8,128)} %copy-done.2), kind=kOutput, calls=%fused_computation.29 | convolution fusion | flops 1360781312 | bytes 21233664 | tf_op jit(solution)/shard_map/ax,nmxc->nmac/dot_general | solution.py:50
  640.7 4.7 constant_dynamic-slice_fusion.7
  645.5 4.8 slice_bitcast_fusion.15
  650.2 2.5 slice_bitcast_fusion.13
  652.7 3.1 slice_bitcast_fusion.11
  655.9 3.1 slice_bitcast_fusion.9
  659.0 2.3 slice_bitcast_fusion.7
  661.3 0.8 slice_bitcast_fusion.5
  662.1 0.8 slice_bitcast_fusion.3
  663.0 0.8 slice_bitcast_fusion.1
  663.8 0.8 copy-done.12
  664.7 3.7 subtract_reduce_fusion.7
  669.1 1.0 copy-done.11
  670.2 3.3 subtract_reduce_fusion.6
  674.2 0.9 copy-done.9
  675.2 0.7 copy-done.10
  676.0 3.3 subtract_reduce_fusion.5
  680.0 0.9 copy-done.7
  680.9 0.7 copy-done.8
  681.7 3.3 subtract_reduce_fusion.4
  685.7 1.0 copy-done.6
  686.8 3.5 subtract_reduce_fusion.3
  691.3 3.3 subtract_reduce_fusion.2
  695.6 3.3 subtract_reduce_fusion.1
  699.6 3.5 subtract_reduce_fusion
  703.9 4.8 fusion.21
  708.7 2.3 fusion.13
  711.0 2.4 fusion.40
  713.5 2.8 copy.17
  716.3 69.5 %reduce-scatter.2.cloned.1.call-done = f32[4,8,9,128]{3,1,2,0:T(8,128)} async-done(((f32[64,8,9,128]{3,1,2,0:T(8,128)}), f32[4,8,9,128]{3,1,2,0:T(8,128)}) %reduce-scatter.2.cloned.1.call-update) | async-done | bytes 147472 | tf_op jit(solution)/shard_map/reduce_scatter | solution.py:109
  (76 shorter events, 9.1 us)
Async XLA Ops:
  6.5 508.6 %copy-start = (bf16[8,9,64,128]{3,2,1,0:T(8,128)(2,1)S(1)}, bf16[8,9,64,128]{3,2,1,0:T(8,128)(2,1)}, u32[]{:S(2)}) copy-start(bf16[8,9,64,128]{3,2,1,0:T(8,128)(2,1)} %param.6) | copy-start | bytes 3538948
  6.5 779.2 %reduce-scatter.2.cloned.1.call-start = ((), (), s32[]{:S(2)}) async-start(), calls=%async_computation.2 | async-start | bytes 2506752 | tf_op jit(solution)/shard_map/reduce_scatter | solution.py:109
  70.5 10.5 %copy-start.31 = (s32[16]{0:T(128)S(1)}, s32[16]{0:T(128)}, u32[]{:S(2)}) copy-start(s32[16]{0:T(128)} %param.8) | copy-start | bytes 196
  74.0 107.4 %collective-permute-start = (bf16[4,8,9,64,128]{4,1,3,2,0:T(8,128)(2,1)}, bf16[4,8,9,64,128]{4,1,3,2,0:T(8,128)(2,1)}, u32[]{:S(2)}, u32[]{:S(2)}) collective-permute-start(bf16[4,8,9,64,128]{4,1,3,2,0:T(8,128)(2,1)} %bitcast.4), channel_id=1, source_target_pairs={{0,112},{16,0},{32,16},{48,32},{64,48},{80,64},{96,80},{112,96},{1... | collective-permute-start | bytes 14155784 | tf_op jit(solution)/shard_map/ppermute | solution.py:12
  186.3 102.5 %collective-permute-start.1 = (bf16[4,8,9,64,128]{4,1,3,2,0:T(8,128)(2,1)}, bf16[4,8,9,64,128]{4,1,3,2,0:T(8,128)(2,1)}, u32[]{:S(2)}, u32[]{:S(2)}) collective-permute-start(bf16[4,8,9,64,128]{4,1,3,2,0:T(8,128)(2,1)} %broadcast_select_fusion), channel_id=1, source_target_pairs={{0,96},{16,112},{32,0},{48,16},{64,32},{80,48},{96,64},{112,80},{1... | collective-permute-start | bytes 14155784 | tf_op jit(solution)/shard_map/ppermute | solution.py:12
  293.8 103.1 %collective-permute-start.2 = (bf16[4,8,9,64,128]{4,1,3,2,0:T(8,128)(2,1)}, bf16[4,8,9,64,128]{4,1,3,2,0:T(8,128)(2,1)}, u32[]{:S(2)}, u32[]{:S(2)}) collective-permute-start(bf16[4,8,9,64,128]{4,1,3,2,0:T(8,128)(2,1)} %broadcast_select_fusion.1), channel_id=1, source_target_pairs={{0,64},{16,80},{32,96},{48,112},{64,0},{80,16},{96,32},{112,48},{1... | collective-permute-start | bytes 14155784 | tf_op jit(solution)/shard_map/ppermute | solution.py:12
  295.3 218.5 %copy-start.29 = (f32[8,8]{1,0:T(8,128)S(1)}, f32[8,8]{1,0:T(8,128)}, u32[]{:S(2)}) copy-start(f32[8,8]{1,0:T(8,128)} %param.7) | copy-start | bytes 772
  399.8 2.2 copy-start.13
  402.0 105.2 %collective-permute-start.3 = (bf16[4,8,9,64,128]{4,1,3,2,0:T(8,128)(2,1)S(1)}, bf16[4,8,9,64,128]{4,1,3,2,0:T(8,128)(2,1)}, u32[]{:S(2)}, u32[]{:S(2)}) collective-permute-start(bf16[4,8,9,64,128]{4,1,3,2,0:T(8,128)(2,1)S(1)} %broadcast_select_fusion.2), channel_id=1, source_target_pairs={{0,112},{16,0},{32,16},{48,32},{64,48},{80,64},{96,80},{112,96},{1... | collective-permute-start | bytes 14155784 | tf_op jit(solution)/shard_map/ppermute | solution.py:12
  507.2 103.9 %collective-permute-start.4 = (bf16[4,8,9,64,128]{4,1,3,2,0:T(8,128)(2,1)}, bf16[4,8,9,64,128]{4,1,3,2,0:T(8,128)(2,1)}, u32[]{:S(2)}, u32[]{:S(2)}) collective-permute-start(bf16[4,8,9,64,128]{4,1,3,2,0:T(8,128)(2,1)} %collective-permute-done.3), channel_id=1, source_target_pairs={{0,112},{16,0},{32,16},{48,32},{64,48},{80,64},{96,80},{112,96},{1... | collective-permute-start | bytes 14155784 | tf_op jit(solution)/shard_map/ppermute | solution.py:12
  515.2 2.1 copy-start.27
  618.9 5.1 copy-start.2
  645.5 4.8 copy-start.5
  650.2 2.5 copy-start.4
  652.7 3.2 copy-start.3
  663.0 1.7 copy-start.12
  663.0 1.7 copy-start.25
  663.0 1.7 copy-start.26
  668.4 1.7 copy-start.11
  668.4 1.7 copy-start.23
  668.4 1.7 copy-start.24
  673.5 1.7 copy-start.9
  673.5 2.4 copy-start.10
  673.5 2.4 copy-start.21
  673.5 2.4 copy-start.22
  679.3 1.7 copy-start.7
  679.3 2.4 copy-start.8
  679.3 2.4 copy-start.19
  679.3 2.4 copy-start.20
  685.0 1.7 copy-start.6
  685.0 1.7 copy-start.17
  685.1 1.7 copy-start.18
  690.3 1.0 copy-start.15
  690.3 1.0 copy-start.16
  694.6 1.0 copy-start.14
  703.1 0.8 copy-start.28
  703.1 0.8 copy-start.30
  713.5 72.3 %copy-start.1 = (bf16[8,9,64,128]{3,2,1,0:T(8,128)(2,1)S(1)}, bf16[8,9,64,128]{3,2,1,0:T(8,128)(2,1)}, u32[]{:S(2)}) copy-start(bf16[8,9,64,128]{3,2,1,0:T(8,128)(2,1)} %param.6) | copy-start | bytes 3538948
Sparse Core Ops, SparseCore 0:
  716.4 69.3 reduce-scatter.1
